TPU v7x, 32 devices: a whole 2x2x4 slice. The times are simulated.
32 devices in a mesh: ia: 2 (over y), ja: 4 (over z), ka: 4 (over x, core).
Axes of the slice: x: 2, y: 2, z: 4, core: 2. Of those that a mesh axis runs over, the one named last changes fastest.
Arguments:
- blocks: bfloat16 [256, 64, 4096], P(('ia', 'ja', 'ka')), may hold values from -12 to 12
- coords: int32 [256, 3], P(('ia', 'ja', 'ka')), may hold values from 0 to 63, as said below
- factor_one: float32 [2048, 512], P('ia'), may hold values from -1.2 to 1.2
- factor_two: float32 [4096, 512], P('ja'), may hold values from -1.2 to 1.2
- factor_three: float32 [4096, 512], P('ka'), may hold values from -1.2 to 1.2
Outputs:
- swept_one: float32 [2048, 512], P('ia')
- swept_two: float32 [4096, 512], P('ja')
- swept_three: float32 [4096, 512], P('ka')
Inputs may be any that keep to these rules, and one draw needn't show every extreme that they name: Row n of coords holds the three block coordinates of block n. The 8 rows of one device of ia+ja+ka (aligned blocks of 8 rows, devices in the order ia, ja, ka) have their second coordinate within that device's ja range (16 * ja to 16 * ja + 15) and their third within its ka range; at most 8 of them have a first coordinate within any one index of ia's range of 16; in every group of devices that share ja and ka, some index of ia receives exactly 8 from each device of the group. The same block may be listed more than once.
All inputs are finite; a program needn't handle non-finite values.
Results may differ from a plain program's by a relative error of at most 0.0028.
Values may be sent and summed in bfloat16 or wider, within the bound.
A program may use at most 64 MiB of HBM per device.

v0:
```python
import jax
import jax.numpy as jnp
from jax import lax
from jax.sharding import PartitionSpec as P

STEP_SIZE = 0.01
einsum_forms = (
    ("qk,rk->qrk", "pk,qrk->pqr", "pqr,qrk->pk"),
    ("pk,rk->prk", "qk,prk->pqr", "pqr,prk->qk"),
    ("pk,qk->pqk", "rk,pqk->pqr", "pqr,pqk->rk"),
)
other_modes = ((1, 2), (0, 2), (0, 1))


def block_gradient(cube, rows, mode):
    first, second = other_modes[mode]
    outer_form, model_form, grad_form = einsum_forms[mode]
    khatri = jnp.einsum(
        outer_form, rows[first].astype(jnp.float32), rows[second].astype(jnp.float32)
    ).astype(jnp.bfloat16)
    model = jnp.einsum(model_form, rows[mode], khatri, preferred_element_type=jnp.float32)
    misfit = (cube.astype(jnp.float32) - model).astype(jnp.bfloat16)
    return jnp.einsum(grad_form, misfit, khatri, preferred_element_type=jnp.float32)


def accumulate(blocks, coords, factors, starts, live, mode, height):
    edge = blocks.shape[1]
    width = factors[0].shape[1]

    def visit(index, total):

        def add(running):
            place = coords[index]
            rows = tuple(
                (
                    lax.dynamic_slice_in_dim(factors[f], place[f] * edge - starts[f], edge, 0)
                    for f in range(3)
                )
            )
            cube = blocks[index].reshape(edge, edge, edge)
            term = block_gradient(cube, rows, mode)
            offset = place[mode] * edge - starts[mode]
            current = lax.dynamic_slice_in_dim(running, offset, edge, 0)
            return lax.dynamic_update_slice_in_dim(running, current + term, offset, 0)

        return lax.cond(live[index], add, lambda running: running, total)

    empty = jnp.zeros((height, width), jnp.float32)
    return lax.fori_loop(0, blocks.shape[0], visit, empty)


def block_slots(coords, count, per_pair, held_rows):
    target = coords[:, 0] // held_rows
    same = target[:, None] == target[None, :]
    earlier = jnp.arange(count)[None, :] < jnp.arange(count)[:, None]
    before = jnp.sum((same & earlier).astype(jnp.int32), axis=1)
    return target * per_pair + before


def serve_rows(incoming, factor, edge, held_rows):
    width = factor.shape[1]
    within = incoming - lax.axis_index("ia") * held_rows
    safe_rows = jnp.clip(within, 0, held_rows - 1)
    picked = factor.astype(jnp.bfloat16).reshape(held_rows, edge, width)[safe_rows]
    return lax.all_to_all(picked, "ia", split_axis=0, concat_axis=0, tiled=True)


def per_device(blocks, coords, factor_one, factor_two, factor_three):
    edge = blocks.shape[1]
    count = blocks.shape[0]
    groups = lax.axis_size("ia")
    span_one = factor_one.shape[0]
    span_two = factor_two.shape[0]
    span_three = factor_three.shape[0]
    width = factor_one.shape[1]
    held_rows = span_one // edge
    per_pair = max(2, 2 * count // groups)
    start_two = lax.axis_index("ja") * span_two
    start_three = lax.axis_index("ka") * span_three
    slot = block_slots(coords, count, per_pair, held_rows)
    all_slots = groups * per_pair
    wanted = jnp.full((all_slots,), -1, jnp.int32).at[slot].set(coords[:, 0])
    incoming = lax.all_to_all(wanted, "ia", split_axis=0, concat_axis=0, tiled=True)
    fetched = serve_rows(incoming, factor_one, edge, held_rows).reshape(all_slots * edge, width)
    places = coords.at[:, 0].set(slot)
    live = jnp.ones((count,), jnp.bool_)
    slot_terms = accumulate(
        blocks,
        places,
        (fetched, factor_two.astype(jnp.bfloat16), factor_three.astype(jnp.bfloat16)),
        (0, start_two, start_three),
        live,
        0,
        all_slots * edge,
    )
    returned = lax.all_to_all(
        slot_terms.reshape(all_slots, edge, width), "ia", split_axis=0, concat_axis=0, tiled=True
    )
    within = incoming - lax.axis_index("ia") * held_rows
    selector = (within[None, :] == jnp.arange(held_rows)[:, None]).astype(jnp.float32)
    first_part = jnp.dot(
        selector,
        returned.reshape(all_slots, edge * width),
        precision=lax.Precision.HIGHEST,
        preferred_element_type=jnp.float32,
    ).reshape(span_one, width)
    first_part = lax.psum(first_part, ("ja", "ka"))
    factor_one = factor_one + STEP_SIZE * first_part
    first_rows = serve_rows(incoming, factor_one, edge, held_rows).reshape(
        groups * per_pair * edge, width
    )
    first_start = 0
    second_part = accumulate(
        blocks,
        places,
        (first_rows, factor_two.astype(jnp.bfloat16), factor_three.astype(jnp.bfloat16)),
        (first_start, start_two, start_three),
        live,
        1,
        span_two,
    )
    second_part = lax.psum(second_part, ("ia", "ka"))
    factor_two = factor_two + STEP_SIZE * second_part
    third_part = accumulate(
        blocks,
        places,
        (first_rows, factor_two.astype(jnp.bfloat16), factor_three.astype(jnp.bfloat16)),
        (first_start, start_two, start_three),
        live,
        2,
        span_three,
    )
    third_part = lax.psum(third_part, ("ia", "ja"))
    factor_three = factor_three + STEP_SIZE * third_part
    return (factor_one, factor_two, factor_three)


def solution(mesh):
    in_specs = (
        P(("ia", "ja", "ka"), None, None),
        P(("ia", "ja", "ka"), None),
        P("ia", None),
        P("ja", None),
        P("ka", None),
    )
    out_specs = (P("ia", None), P("ja", None), P("ka", None))
    return jax.shard_map(
        per_device, mesh=mesh, in_specs=in_specs, out_specs=out_specs, check_vma=False
    )
```

profile of v0, /device:TPU:0, one launch (start us, length us, event | category | flops | bytes accessed | tf_op | source)
XLA Modules:
  0.0 621.7 jit_solution(2798835930513432250)
XLA Ops:
  10.6 4.3 all-to-all-start
  27.9 8.9 %all-to-all-done.1 = bf16[16,64,512]{2,1,0:T(8,128)(2,1)S(1)} async-done(((bf16[16,64,512]{2,1,0:T(8,128)(2,1)}), bf16[16,64,512]{2,1,0:T(8,128)(2,1)S(1)}, u32[]{:S(2)}, u32[]{:S(2)}) %all-to-all-start.1) | async-done | bytes 1048608 | tf_op jit(solution)/shard_map/all_to_all | solution.py:65
  38.3 86.3 %while.40 = (s32[]{:T(128)}, f32[1024,512]{1,0:T(8,128)}, s32[8,3]{0,1:T(4,128)S(1)}, bf16[8,64,4096]{2,1,0:T(8,128)(2,1)}, bf16[1024,512]{1,0:T(8,128)(2,1)S(1)...) while((s32[]{:T(128)}, f32[1024,512]{1,0:T(8,128)}, ...), condition=%wide.region_4.5_spmd, body=%wide.region_3.4_spmd.sunk | while | flops 546144256 | bytes 15402399 | solution.py:49
  44.1 5.0 fusion.118
  54.8 5.0 fusion.118
  65.6 5.0 fusion.118
  76.4 5.0 fusion.118
  87.2 5.0 fusion.118
  98.0 5.0 fusion.118
  108.8 5.0 fusion.118
  119.6 5.0 fusion.118
  128.5 23.1 %all-to-all-done.2 = f32[16,64,512]{2,1,0:T(8,128)S(1)} async-done(((f32[16,64,512]{2,1,0:T(8,128)}), f32[16,64,512]{2,1,0:T(8,128)S(1)}, u32[]{:S(2)}, u32[]{:S(2)}) %all-to-all-start.2) | async-done | bytes 2097184 | tf_op jit(solution)/shard_map/all_to_all | solution.py:96
  155.5 98.7 %all-reduce.4.cloned.1.call-done = f32[1024,512]{1,0:T(8,128)} async-done(((f32[1024,512]{1,0:T(8,128)}), f32[1024,512]{1,0:T(8,128)}) %all-reduce.4.cloned.1.call-update) | async-done | bytes 2097168 | tf_op jit(solution)/shard_map/psum | solution.py:107
  259.3 4.4 all-to-all-start.3
  263.9 12.9 %all-to-all-done.3 = bf16[16,64,512]{2,1,0:T(8,128)(2,1)} async-done(((bf16[16,64,512]{2,1,0:T(8,128)(2,1)}), bf16[16,64,512]{2,1,0:T(8,128)(2,1)}, u32[]{:S(2)}, u32[]{:S(2)}) %all-to-all-start.3) | async-done | bytes 1048608 | tf_op jit(solution)/shard_map/all_to_all | solution.py:65
  278.4 92.2 %while.41 = (s32[]{:T(128)}, f32[1024,512]{1,0:T(8,128)}, s32[8,3]{0,1:T(4,128)S(1)}, s32[]{:T(128)}, bf16[8,64,4096]{2,1,0:T(8,128)(2,1)}, /*index=5*/s32[]{:T(...) while((s32[]{:T(128)}, f32[1024,512]{1,0:T(8,128)}, ...), condition=%wide.region_7.8_spmd, body=%wide.region_6.7_spmd.sunk | while | flops 546144256 | bytes 9110887 | solution.py:49
  285.6 4.4 fusion.123
  297.1 4.4 fusion.123
  308.6 4.4 fusion.123
  320.1 4.4 fusion.123
  331.6 4.4 fusion.123
  343.2 4.4 fusion.123
  354.7 4.4 fusion.123
  366.2 4.4 fusion.123
  370.6 59.9 %all-reduce.6.cloned.1.call-done = f32[1024,512]{1,0:T(8,128)} async-done(((f32[1024,512]{1,0:T(8,128)}), f32[1024,512]{1,0:T(8,128)}) %all-reduce.6.cloned.1.call-update) | async-done | bytes 2097168 | tf_op jit(solution)/shard_map/psum | solution.py:122
  435.6 74.6 %while.42 = (s32[]{:T(128)}, f32[1024,512]{1,0:T(8,128)}, s32[8,3]{0,1:T(4,128)S(1)}, s32[]{:T(128)}, bf16[8,64,4096]{2,1,0:T(8,128)(2,1)}, /*index=5*/s32[]{:T(...) while((s32[]{:T(128)}, f32[1024,512]{1,0:T(8,128)}, ...), condition=%wide.region_10.11_spmd, body=%wide.region_9.10_spmd.sunk | while | flops 546144256 | bytes 15402399 | solution.py:49
  469.1 3.8 fusion.128
  478.4 3.8 fusion.128
  487.7 3.8 fusion.128
  497.0 3.8 fusion.128
  506.4 3.8 fusion.128
  510.2 101.5 %all-reduce.8.cloned.1.call-done = f32[1024,512]{1,0:T(8,128)} async-done(((f32[1024,512]{1,0:T(8,128)}), f32[1024,512]{1,0:T(8,128)}) %all-reduce.8.cloned.1.call-update) | async-done | bytes 2097168 | tf_op jit(solution)/shard_map/psum | solution.py:133
  (240 shorter events, 152.5 us)
Async XLA Ops:
  10.6 8.0 %all-to-all-start = ((s32[2,8,1]{1,2,0:T(1,128)}), s32[2,8,1]{1,2,0:T(1,128)S(1)}, u32[]{:S(2)}, u32[]{:S(2)}) async-start(s32[2,8,1]{1,2,0:T(1,128)} %bitcast.29), calls=%async_computation | async-start | bytes 2048 | tf_op jit(solution)/shard_map/all_to_all | solution.py:83
  20.3 16.5 %all-to-all-start.1 = ((bf16[16,64,512]{2,1,0:T(8,128)(2,1)}), bf16[16,64,512]{2,1,0:T(8,128)(2,1)S(1)}, u32[]{:S(2)}, u32[]{:S(2)}) async-start(bf16[16,64,512]{2,1,0:T(8,128)(2,1)} %gather_fusion), calls=%async_computation.1 | async-start | bytes 2097152 | tf_op jit(solution)/shard_map/all_to_all | solution.py:65
  44.1 5.1 copy-start.7
  49.1 3.8 copy-start.6
  54.8 5.1 copy-start.7
  59.9 3.8 copy-start.6
  65.6 5.1 copy-start.7
  70.7 3.8 copy-start.6
  76.4 5.1 copy-start.7
  81.5 3.8 copy-start.6
  87.2 5.1 copy-start.7
  92.3 3.8 copy-start.6
  98.0 5.1 copy-start.7
  103.0 3.8 copy-start.6
  108.8 5.1 copy-start.7
  119.6 5.1 copy-start.7
  124.6 27.0 %all-to-all-start.2 = ((f32[16,64,512]{2,1,0:T(8,128)}), f32[16,64,512]{2,1,0:T(8,128)S(1)}, u32[]{:S(2)}, u32[]{:S(2)}) async-start(f32[16,64,512]{2,1,0:T(8,128)} %bitcast.175), calls=%async_computation.2 | async-start | bytes 4194304 | tf_op jit(solution)/shard_map/all_to_all | solution.py:96
  128.4 125.9 %all-reduce.4.cloned.1.call-start = ((), (), s32[]{:S(2)}) async-start(), calls=%async_computation.4 | async-start | bytes 4194304 | tf_op jit(solution)/shard_map/psum | solution.py:107
  155.5 98.8 %copy-start = (f32[1024,512]{1,0:T(8,128)S(1)}, f32[1024,512]{1,0:T(8,128)}, u32[]{:S(2)}) copy-start(f32[1024,512]{1,0:T(8,128)} %param.15) | copy-start | bytes 6291460
  259.3 17.6 %all-to-all-start.3 = ((bf16[16,64,512]{2,1,0:T(8,128)(2,1)}), bf16[16,64,512]{2,1,0:T(8,128)(2,1)}, u32[]{:S(2)}, u32[]{:S(2)}) async-start(bf16[16,64,512]{2,1,0:T(8,128)(2,1)} %gather_fusion.1), calls=%async_computation.3 | async-start | bytes 2097152 | tf_op jit(solution)/shard_map/all_to_all | solution.py:65
  263.7 166.9 %all-reduce.6.cloned.1.call-start = ((), (), s32[]{:S(2)}) async-start(), calls=%async_computation.5 | async-start | bytes 4194304 | tf_op jit(solution)/shard_map/psum | solution.py:122
  370.6 60.0 %copy-start.2 = (f32[1024,512]{1,0:T(8,128)S(1)}, f32[1024,512]{1,0:T(8,128)}, u32[]{:S(2)}) copy-start(f32[1024,512]{1,0:T(8,128)} %param.16) | copy-start | bytes 6291460
  370.6 241.1 %all-reduce.8.cloned.1.call-start = ((), (), s32[]{:S(2)}) async-start(), calls=%async_computation.6 | async-start | bytes 4194304 | tf_op jit(solution)/shard_map/psum | solution.py:133
  441.1 3.8 copy-start.5
  450.4 3.8 copy-start.5
  459.7 3.8 copy-start.5
  469.0 3.8 copy-start.5
  478.4 3.8 copy-start.5
  487.7 3.8 copy-start.5
  497.0 3.8 copy-start.5
  506.4 3.8 copy-start.5
  510.2 101.5 %copy-start.3 = (f32[1024,512]{1,0:T(8,128)S(1)}, f32[1024,512]{1,0:T(8,128)}, u32[]{:S(2)}) copy-start(f32[1024,512]{1,0:T(8,128)} %param.17) | copy-start | bytes 6291460
  (11 other events, 38.6 us)
Sparse Core Ops, SparseCore 0:
  155.6 98.5 all-reduce.3
  370.7 59.7 all-reduce.5
  510.3 101.3 all-reduce.7
where the time goes:
time: 626 us; the launch traced here: 622 us
  waiting for transfers between devices  307 us (49%)
  matrix products  107 us (17%)
  other arithmetic  65.5 us (10%)
  local copies, waits for them, and re-layouts  64.8 us (10%)
  loops' own time  47.1 us (8%)
  starting transfers between devices  16.3 us (3%)
  between operations  13.8 us (2%)
    dot_general x24, matrix products, block_gradient(): jnp.einsum(grad_form, misfit, khatri, preferred_element_type=jnp.float32)  106 us
    psum x1, waiting for transfers between devices, per_device(): third_part = lax.psum(third_part, ('ia', 'ja'))  102 us
    psum x1, waiting for transfers between devices, per_device(): first_part = lax.psum(first_part, ('ja', 'ka'))  98.7 us
    psum x1, waiting for transfers between devices, per_device(): second_part = lax.psum(second_part, ('ia', 'ka'))  59.9 us
    another operation x3, loops' own time, accumulate(): return lax.fori_loop(0, blocks.shape[0], visit, empty)  47.1 us
    convert_element_type x32, local copies, waits for them, and re-layouts, block_gradient(): misfit = (cube.astype(jnp.float32) - model).astype(jnp.bfloat16)  34.5 us
    convert_element_type x24, other arithmetic, block_gradient(): misfit = (cube.astype(jnp.float32) - model).astype(jnp.bfloat16)  26.8 us
    all_to_all x1, waiting for transfers between devices, per_device(): lax.all_to_all(slot_terms.reshape(all_slots, edge, width), 'ia', split_ax...  23.1 us
  transfers between devices with their start and end apart: 7, of which 7 were waited for; matrix products, arithmetic and copies ran while one was open for 1% of the time, Pallas kernels for 0%

commit v1 on v0

v1 whole, which is shorter than its diff:
```python
import functools

import jax
import jax.numpy as jnp
from jax import lax
from jax.experimental import pallas as pl
from jax.experimental.pallas import tpu as pltpu
from jax.sharding import PartitionSpec as P

STEP_SIZE = 0.01
F32 = jnp.float32
BF16 = jnp.bfloat16


def gradient_kernel(mode, group, place_ref, x_ref, one_ref, two_ref, three_ref, out_ref, acc, term, three_pad):
    step = pl.program_id(0)
    edge, width = one_ref.shape
    lanes = group * edge

    @pl.when(step == 0)
    def _():
        acc[...] = jnp.zeros_like(acc)

    one = one_ref[...].astype(BF16)
    two = two_ref[...].astype(BF16)
    three = three_ref[...].astype(BF16)
    two_wide = two.astype(F32)
    if mode == 1:
        one_wide = one.astype(F32)
        three_pad[...] = jnp.zeros_like(three_pad)
        three_pad[0, :edge, :] = three
        three_pad[1, edge:, :] = three
    else:
        term[...] = jnp.zeros_like(term)
    for c in range(edge // group):
        kr = jnp.concatenate(
            [
                jnp.broadcast_to(two_wide[q : q + 1, :], (edge, width)).astype(BF16) * three
                for q in range(c * group, (c + 1) * group)
            ],
            axis=0,
        )
        model = lax.dot_general(one, kr, (((1,), (1,)), ((), ())), preferred_element_type=F32)
        misfit = (x_ref[0, :, c * lanes : (c + 1) * lanes].astype(F32) - model).astype(BF16)
        if mode == 0:
            term[...] += jnp.dot(misfit, kr, preferred_element_type=F32)
        elif mode == 1:
            for pair in range(group // 2):
                both = misfit[:, pair * 2 * edge : (pair + 1) * 2 * edge]
                for half in range(2):
                    mixed = jnp.dot(both, three_pad[half], preferred_element_type=F32)
                    q = c * group + 2 * pair + half
                    term[q : q + 1, :] = jnp.sum(mixed * one_wide, axis=0, keepdims=True)
        else:
            mixed = lax.dot_general(misfit, one, (((0,), (0,)), ((), ())), preferred_element_type=F32)
            total = None
            for g in range(group):
                q = c * group + g
                part = mixed[g * edge : (g + 1) * edge, :] * two_wide[q : q + 1, :]
                total = part if total is None else total + part
            term[...] += total
    offset = pl.multiple_of(place_ref[step, mode] * edge, edge)
    acc[pl.ds(offset, edge), :] += term[...]

    @pl.when(step == pl.num_programs(0) - 1)
    def _():
        out_ref[...] = acc[...].astype(out_ref.dtype)


def accumulate(blocks, places, factors, mode, height):
    count, edge, _ = blocks.shape
    width = factors[0].shape[1]
    row_spec = lambda f: pl.BlockSpec((edge, width), lambda i, place: (place[i, f], 0))
    flops = 4 * count * edge**3 * width
    return pl.pallas_call(
        functools.partial(gradient_kernel, mode, 8),
        grid_spec=pltpu.PrefetchScalarGridSpec(
            num_scalar_prefetch=1,
            grid=(count,),
            in_specs=[
                pl.BlockSpec((1, edge, edge * edge), lambda i, place: (i, 0, 0)),
                row_spec(0),
                row_spec(1),
                row_spec(2),
            ],
            out_specs=pl.BlockSpec((height, width), lambda i, place: (0, 0)),
            scratch_shapes=[
                pltpu.VMEM((height, width), F32),
                pltpu.VMEM((edge, width), F32),
                pltpu.VMEM((2, 2 * edge, width), BF16),
            ],
        ),
        out_shape=jax.ShapeDtypeStruct((height, width), BF16),
        cost_estimate=pl.CostEstimate(flops=flops, bytes_accessed=2 * blocks.size, transcendentals=0),
        name=f"gradient{mode}",
    )(places, blocks, *factors)


def block_slots(coords, count, per_pair, held_rows):
    target = coords[:, 0] // held_rows
    same = target[:, None] == target[None, :]
    earlier = jnp.arange(count)[None, :] < jnp.arange(count)[:, None]
    before = jnp.sum((same & earlier).astype(jnp.int32), axis=1)
    return target * per_pair + before


def serve_rows(incoming, factor, edge, held_rows):
    width = factor.shape[1]
    within = incoming - lax.axis_index("ia") * held_rows
    safe_rows = jnp.clip(within, 0, held_rows - 1)
    picked = factor.astype(BF16).reshape(held_rows, edge, width)[safe_rows]
    return lax.all_to_all(picked, "ia", split_axis=0, concat_axis=0, tiled=True)


def per_device(blocks, coords, factor_one, factor_two, factor_three):
    count, edge, _ = blocks.shape
    groups = lax.axis_size("ia")
    span_one, width = factor_one.shape
    span_two = factor_two.shape[0]
    span_three = factor_three.shape[0]
    held_rows = span_one // edge
    per_pair = max(2, 2 * count // groups)
    slot = block_slots(coords, count, per_pair, held_rows)
    all_slots = groups * per_pair
    wanted = jnp.full((all_slots,), -1, jnp.int32).at[slot].set(coords[:, 0])
    incoming = lax.all_to_all(wanted, "ia", split_axis=0, concat_axis=0, tiled=True)
    fetched = serve_rows(incoming, factor_one, edge, held_rows).reshape(all_slots * edge, width)
    places = jnp.stack(
        [
            slot,
            coords[:, 1] - lax.axis_index("ja") * (span_two // edge),
            coords[:, 2] - lax.axis_index("ka") * (span_three // edge),
        ],
        axis=1,
    )
    slot_terms = accumulate(blocks, places, (fetched, factor_two, factor_three), 0, all_slots * edge)
    returned = lax.all_to_all(
        slot_terms.reshape(all_slots, edge, width), "ia", split_axis=0, concat_axis=0, tiled=True
    )
    within = incoming - lax.axis_index("ia") * held_rows
    selector = (within[None, :] == jnp.arange(held_rows)[:, None]).astype(BF16)
    first_part = jnp.dot(
        selector,
        returned.reshape(all_slots, edge * width),
        preferred_element_type=F32,
    ).reshape(span_one, width)
    first_part = lax.psum(first_part, ("ja", "ka"))
    factor_one = factor_one + STEP_SIZE * first_part
    first_rows = serve_rows(incoming, factor_one, edge, held_rows).reshape(all_slots * edge, width)
    second_part = accumulate(blocks, places, (first_rows, factor_two, factor_three), 1, span_two)
    factor_two = factor_two + STEP_SIZE * lax.psum(second_part.astype(F32), ("ia", "ka"))
    third_part = accumulate(blocks, places, (first_rows, factor_two, factor_three), 2, span_three)
    factor_three = factor_three + STEP_SIZE * lax.psum(third_part.astype(F32), ("ia", "ja"))
    return (factor_one, factor_two, factor_three)


def solution(mesh):
    in_specs = (
        P(("ia", "ja", "ka"), None, None),
        P(("ia", "ja", "ka"), None),
        P("ia", None),
        P("ja", None),
        P("ka", None),
    )
    out_specs = (P("ia", None), P("ja", None), P("ka", None))
    return jax.shard_map(
        per_device, mesh=mesh, in_specs=in_specs, out_specs=out_specs, check_vma=False
    )
```

time: 626 us -> 426 us (0.68)
  waiting for transfers between devices: 307 us -> 125 us
  blocking collectives: 0 us -> 164 us
  matrix products: 107 us -> 0.42 us
  Pallas kernels: 0 us -> 88.8 us
  local copies, waits for them, and re-layouts: 64.8 us -> 7.8 us
  other arithmetic: 65.5 us -> 13.8 us
  loops' own time: 47.1 us -> 0 us
    psum x2 -> x0, waiting for transfers between devices: 161 us -> none  [the longest x1 102 us: per_device(): third_part = lax.psum(third_part, ('ia', 'ja'))]
    psum x0 -> x2, blocking collectives: none -> 148 us  [the longest x1 91.4 us: per_device(): lax.psum(third_part.astype(F32), ('ia', 'ja'))]
    dot_general x25 -> x1, matrix products: 107 us -> 0.42 us  [per_device(): jnp.dot(selector, returned.reshape(all_slots, edge * width), preferred_el...]
    pallas_call x0 -> x3, Pallas kernels: none -> 88.8 us  [accumulate(): pl.pallas_call(functools.partial(gradient_kernel, mode, 8), grid_spec=plt...]
    another operation x3 -> x0, loops' own time: 47.1 us -> none  [accumulate(): return lax.fori_loop(0, blocks.shape[0], visit, empty)]
    convert_element_type x32 -> x0, local copies, waits for them, and re-layouts: 34.5 us -> none  [block_gradient(): misfit = (cube.astype(jnp.float32) - model).astype(jnp.bfloat16)]
    convert_element_type x29 -> x2, other arithmetic: 39.3 us -> 5.14 us  [serve_rows(): picked = factor.astype(BF16).reshape(held_rows, edge, width)[safe_rows]]
    another operation x25 -> x1, other arithmetic: 21.9 us -> 0.67 us  [per_device(): jnp.stack([slot, coords[:, 1] - lax.axis_index('ja') * (span_two // edge)...]
  transfers between devices with their start and end apart: 7 -> 4, of which waited for: 7 -> 4; matrix products, arithmetic and copies ran while one was open for 1% -> 1% of each run, Pallas kernels for 0% -> 0%
where the time goes in v1:
time: 426 us; the launch traced here: 425 us
  blocking collectives  164 us (38%)
  waiting for transfers between devices  125 us (29%)
  Pallas kernels  88.8 us (21%)
  between operations  14.1 us (3%)
  other arithmetic  13.8 us (3%)
  starting transfers between devices  11.5 us (3%)
  local copies, waits for them, and re-layouts  7.8 us (2%)
    psum x1, waiting for transfers between devices, per_device(): first_part = lax.psum(first_part, ('ja', 'ka'))  98.7 us
    psum x1, blocking collectives, per_device(): lax.psum(third_part.astype(F32), ('ia', 'ja'))  91.4 us
    pallas_call x3, Pallas kernels, accumulate(): pl.pallas_call(functools.partial(gradient_kernel, mode, 8), grid_spec=plt...  88.8 us
    psum x1, blocking collectives, per_device(): lax.psum(second_part.astype(F32), ('ia', 'ka'))  56.6 us
    all_to_all x1, blocking collectives, serve_rows(): return lax.all_to_all(picked, 'ia', split_axis=0, concat_axis=0, tiled=True)  16.1 us
    all_to_all x1, waiting for transfers between devices, serve_rows(): return lax.all_to_all(picked, 'ia', split_axis=0, concat_axis=0, tiled=True)  12 us
    all_to_all x1, waiting for transfers between devices, per_device(): lax.all_to_all(slot_terms.reshape(all_slots, edge, width), 'ia', split_ax...  11.9 us
  transfers between devices with their start and end apart: 4, of which 4 were waited for; matrix products, arithmetic and copies ran while one was open for 1% of the time, Pallas kernels for 0%

profile of v1, /device:TPU:0, one launch (start us, length us, event | category | flops | bytes accessed | tf_op | source)
XLA Modules:
  0.0 425.2 jit_solution(12890407098365941194)
XLA Ops:
  7.2 0.7 and_select_fusion
  7.9 0.8 slice_bitcast_fusion
  8.7 0.1 fusion.9
  8.9 0.2 convert_reduce_fusion
  9.1 0.1 fusion.2
  9.3 0.6 scatter_custom_fusion
  9.9 0.6 all_to_all.15
  10.5 4.3 %all-to-all-start = ((s32[2,8,1]{1,2,0:T(1,128)}), s32[2,8,1]{1,2,0:T(1,128)S(1)}, u32[]{:S(2)}, u32[]{:S(2)}) async-start(s32[2,8,1]{1,2,0:T(1,128)} %bitcast.1), calls=%async_computation | async-start | bytes 2048 | tf_op jit(solution)/shard_map/all_to_all | solution.py:126
  14.8 1.7 convert_element_type.17
  16.5 2.0 all-to-all-done
  18.5 0.1 min.14
  18.6 1.6 gather_fusion
  20.2 3.6 all-to-all-start.1
  23.9 0.7 pad_add_fusion.place_ref
  24.6 12.0 %all-to-all-done.1 = bf16[16,64,512]{2,1,0:T(8,128)(2,1)S(1)} async-done(((bf16[16,64,512]{2,1,0:T(8,128)(2,1)}), bf16[16,64,512]{2,1,0:T(8,128)(2,1)S(1)}, u32[]{:S(2)}, u32[]{:S(2)}) %all-to-all-start.1) | async-done | bytes 1048608 | tf_op jit(solution)/shard_map/all_to_all | solution.py:112
  36.6 1.0 copy-done.1
  37.6 25.5 %gradient0.1 = bf16[1024,512]{1,0:T(8,128)(2,1)} custom-call(s32[8,3]{1,0:T(8,128)} %pad_add_fusion.place_ref, bf16[8,64,4096]{2,1,0:T(8,128)(2,1)} %x_ref.5, bf16[1024,512]{1,0:T(8,128)(2,1)} %bitcast.20, f32[1024,512]{1,0:T(8,128)} %two_ref.3, f32[1024,512]{1,0:T(8,128)} %three_ref.5), custom_call_target="tpu_custom_call" | custom-call | flops 4294967296 | bytes 4194304 | tf_op jit(solution)/shard_map/gradient0/pallas_call | solution.py:75
  63.1 3.6 all-to-all-start.2
  66.8 11.9 %all-to-all-done.2 = bf16[16,64,512]{2,1,0:T(8,128)(2,1)S(1)} async-done(((bf16[16,64,512]{2,1,0:T(8,128)(2,1)}), bf16[16,64,512]{2,1,0:T(8,128)(2,1)S(1)}, u32[]{:S(2)}, u32[]{:S(2)}) %all-to-all-start.2) | async-done | bytes 1048608 | tf_op jit(solution)/shard_map/all_to_all | solution.py:137
  78.7 0.6 copy.30
  79.3 0.4 fusion
  79.7 1.5 reshape.97
  81.3 98.7 %all-reduce.4.cloned.1.call-done = f32[1024,512]{1,0:T(8,128)} async-done(((f32[1024,512]{1,0:T(8,128)}), f32[1024,512]{1,0:T(8,128)}) %all-reduce.4.cloned.1.call-update) | async-done | bytes 2097168 | tf_op jit(solution)/shard_map/psum | solution.py:147
  180.0 3.4 fusion.10
  183.4 0.6 gather_fusion.1
  184.0 16.1 %all_to_all.24 = bf16[16,64,512]{2,1,0:T(8,128)(2,1)} all-to-all(bf16[16,64,512]{2,1,0:T(8,128)(2,1)S(1)} %gather_fusion.1), channel_id=1, replica_groups=mesh['ia'=2,'ja'=4,'ka'=4] {'ia'}, dimensions={0} | all-to-all | bytes 2097152 | tf_op jit(solution)/shard_map/all_to_all | solution.py:112
  200.2 31.5 %gradient1.1 = bf16[1024,512]{1,0:T(8,128)(2,1)} custom-call(s32[8,3]{1,0:T(8,128)} %pad_add_fusion.place_ref, bf16[8,64,4096]{2,1,0:T(8,128)(2,1)} %x_ref.5, bf16[1024,512]{1,0:T(8,128)(2,1)} %bitcast.22, f32[1024,512]{1,0:T(8,128)} %two_ref.3, f32[1024,512]{1,0:T(8,128)} %three_ref.5), custom_call_target="tpu_custom_call" | custom-call | flops 4294967296 | bytes 4194304 | tf_op jit(solution)/shard_map/gradient1/pallas_call | solution.py:75
  231.7 56.6 %all-reduce.5 = f32[1024,512]{1,0:T(8,128)S(1)} all-reduce(bf16[1024,512]{1,0:T(8,128)(2,1)} %gradient1.1), channel_id=1, replica_groups=mesh['ia'=2,'ja'=4,'ka'=4] {'ia','ka'}, use_global_device_ids=true, to_apply=%region_3.4 | all-reduce | flops 524288 | bytes 3145728 | tf_op jit(solution)/shard_map/psum | solution.py:151
  288.3 3.4 multiply_add_fusion.1.two_ref
  291.7 31.8 %gradient2.1 = bf16[1024,512]{1,0:T(8,128)(2,1)} custom-call(s32[8,3]{1,0:T(8,128)} %pad_add_fusion.place_ref, bf16[8,64,4096]{2,1,0:T(8,128)(2,1)} %x_ref.5, bf16[1024,512]{1,0:T(8,128)(2,1)} %bitcast.23, f32[1024,512]{1,0:T(8,128)} %multiply_add_fusion.1.two_ref, f32[1024,512]{1,0:T(8,128)} %three_ref.5), custom_call_target="tpu_custom_call" | custom-call | flops 4294967296 | bytes 4194304 | tf_op jit(solution)/shard_map/gradient2/pallas_call | solution.py:75
  323.5 91.4 %all-reduce.6 = f32[1024,512]{1,0:T(8,128)S(1)} all-reduce(bf16[1024,512]{1,0:T(8,128)(2,1)} %gradient2.1), channel_id=1, replica_groups=mesh['ia'=2,'ja'=4,'ka'=4] {'ia','ja'}, use_global_device_ids=true, to_apply=%region_4.5 | all-reduce | flops 524288 | bytes 3145728 | tf_op jit(solution)/shard_map/psum | solution.py:153
  414.9 3.4 multiply_add_fusion
  (14 shorter events, 0.5 us)
Async XLA Ops:
  10.5 8.0 %all-to-all-start = ((s32[2,8,1]{1,2,0:T(1,128)}), s32[2,8,1]{1,2,0:T(1,128)S(1)}, u32[]{:S(2)}, u32[]{:S(2)}) async-start(s32[2,8,1]{1,2,0:T(1,128)} %bitcast.1), calls=%async_computation | async-start | bytes 2048 | tf_op jit(solution)/shard_map/all_to_all | solution.py:126
  20.2 16.5 %all-to-all-start.1 = ((bf16[16,64,512]{2,1,0:T(8,128)(2,1)}), bf16[16,64,512]{2,1,0:T(8,128)(2,1)S(1)}, u32[]{:S(2)}, u32[]{:S(2)}) async-start(bf16[16,64,512]{2,1,0:T(8,128)(2,1)} %gather_fusion), calls=%async_computation.1 | async-start | bytes 2097152 | tf_op jit(solution)/shard_map/all_to_all | solution.py:112
  36.6 1.0 copy-start.1
  63.1 15.6 %all-to-all-start.2 = ((bf16[16,64,512]{2,1,0:T(8,128)(2,1)}), bf16[16,64,512]{2,1,0:T(8,128)(2,1)S(1)}, u32[]{:S(2)}, u32[]{:S(2)}) async-start(bf16[16,64,512]{2,1,0:T(8,128)(2,1)} %bitcast.21), calls=%async_computation.2 | async-start | bytes 2097152 | tf_op jit(solution)/shard_map/all_to_all | solution.py:137
  66.7 113.3 %all-reduce.4.cloned.1.call-start = ((), (), s32[]{:S(2)}) async-start(), calls=%async_computation.4 | async-start | bytes 4194304 | tf_op jit(solution)/shard_map/psum | solution.py:147
  81.2 98.8 %copy-start = (f32[1024,512]{1,0:T(8,128)S(1)}, f32[1024,512]{1,0:T(8,128)}, u32[]{:S(2)}) copy-start(f32[1024,512]{1,0:T(8,128)} %param.7) | copy-start | bytes 6291460
Sparse Core Ops, SparseCore 0:
  81.4 98.5 all-reduce.3
